TPU v7x, 32 devices: a whole 2x2x4 slice. The times are simulated.
32 devices in a mesh: blk: 8 (over y, x, core), uly: 4 (over z).
Axes of the slice: x: 2, y: 2, z: 4, core: 2. Of those that a mesh axis runs over, the one named last changes fastest.
Arguments:
- qkv: bfloat16 [2048, 3, 3072], P(('blk', 'uly')), may hold values from -9 to 9
Outputs:
- attended: float32 [2048, 3072], P('blk', 'uly')
- log_total: float32 [24, 2048], P('uly', 'blk')
All inputs are finite; a program needn't handle non-finite values.
Results may differ from a plain program's by a relative error of at most 0.0027.
Values may be sent and summed in bfloat16 or wider, within the bound.
No kernel may reach another device: no remote copies, remote signals or barrier semaphores. Data moves between devices by JAX's collectives and lax.ppermute only.
A program may use at most 64 MiB of HBM per device.

v0:
```python
import math
import jax
import jax.numpy as jnp
from jax import lax
from jax.sharding import PartitionSpec as P

HEAD_DIM = 128


def from_behind(value, axis, steps):
    count = lax.axis_size(axis)
    pairs = [(source, (source + steps) % count) for source in range(count)]
    return lax.ppermute(value, axis, pairs)


def block_scores(query_rows, key_rows, temper):
    return (
        jnp.einsum("rhd,khd->hrk", query_rows, key_rows, preferred_element_type=jnp.float32)
        * temper
    )


def attend_first(query_rows, key_rows, value_rows, temper):
    scores = block_scores(query_rows, key_rows, temper)
    top = jnp.max(scores, axis=2)
    weights = jnp.exp(scores - top[:, :, None])
    total = jnp.sum(weights, axis=2)
    accum = jnp.einsum(
        "hrk,khd->hrd", weights.astype(jnp.bfloat16), value_rows, preferred_element_type=jnp.float32
    )
    return (top, total, accum)


def attend_next(running, query_rows, key_rows, value_rows, temper):
    top, total, accum = running
    scores = block_scores(query_rows, key_rows, temper)
    newtop = jnp.maximum(top, jnp.max(scores, axis=2))
    factor = jnp.exp(top - newtop)
    weights = jnp.exp(scores - newtop[:, :, None])
    total = total * factor + jnp.sum(weights, axis=2)
    accum = accum * factor[:, :, None] + jnp.einsum(
        "hrk,khd->hrd", weights.astype(jnp.bfloat16), value_rows, preferred_element_type=jnp.float32
    )
    return (newtop, total, accum)


def shards(qkv):
    width = qkv.shape[2] // lax.axis_size("uly")
    heads_local = width // HEAD_DIM
    temper = 1.0 / math.sqrt(HEAD_DIM)
    grouped = lax.all_to_all(qkv, "uly", split_axis=2, concat_axis=0, tiled=True)
    prev_pairs = from_behind(grouped[:, 1:], "blk", 1)
    block_len = grouped.shape[0]
    row_count = math.gcd(block_len, 512)
    queries = grouped[:, 0].reshape(block_len // row_count, row_count, heads_local, HEAD_DIM)
    own_keys = grouped[:, 1].reshape(block_len, heads_local, HEAD_DIM)
    own_values = grouped[:, 2].reshape(block_len, heads_local, HEAD_DIM)
    prev_keys = prev_pairs[:, 0].reshape(block_len, heads_local, HEAD_DIM)
    prev_values = prev_pairs[:, 1].reshape(block_len, heads_local, HEAD_DIM)

    def per_rows(query_rows):
        running = attend_first(query_rows, own_keys, own_values, temper)
        top, total, accum = attend_next(running, query_rows, prev_keys, prev_values, temper)
        normed = accum / total[:, :, None]
        return (jnp.transpose(normed, (1, 0, 2)).reshape(row_count, width), top + jnp.log(total))

    attended_rows, log_rows = lax.map(per_rows, queries)
    attended = attended_rows.reshape(block_len, width)
    log_total = jnp.transpose(log_rows, (1, 0, 2)).reshape(heads_local, block_len)
    return (attended, log_total)


def solution(mesh):
    placed = (P(("blk", "uly"), None, None),)
    return jax.shard_map(
        shards,
        mesh=mesh,
        in_specs=placed,
        out_specs=(P("blk", "uly"), P("uly", "blk")),
        check_vma=False,
    )
```

profile of v0, /device:TPU:0, one launch (start us, length us, event | category | flops | bytes accessed | tf_op | source)
XLA Modules:
  0.0 74.6 jit_solution(17815620228269308837)
XLA Ops:
  0.6 4.6 %copy.32 = bf16[64,3,3072]{0,1,2:T(4,128)(2,1)S(1)} copy(bf16[64,3,3072]{2,0,1:T(8,128)(2,1)} %param.1) | data formatting | bytes 2359296 | tf_op args[0]
  5.2 3.1 %reshape.40 = bf16[4,2,73728]{2,1,0:T(2,128)(2,1)} reshape(bf16[3072,3,64]{2,1,0:T(4,128)(2,1)S(1)} %bitcast.42) | data formatting | bytes 2359296
  8.3 35.0 %all_to_all.18 = bf16[4,2,73728]{2,1,0:T(2,128)(2,1)} all-to-all(bf16[4,2,73728]{2,1,0:T(2,128)(2,1)} %reshape.40), channel_id=1, replica_groups=mesh['blk'=8,'uly'=4] {'uly'}, dimensions={0} | all-to-all | bytes 2359296 | tf_op jit(solution)/shard_map/all_to_all | solution.py:51
  43.2 3.5 %reshape.41 = bf16[3072,3,64]{2,1,0:T(4,128)(2,1)S(1)} reshape(bf16[4,2,73728]{2,1,0:T(2,128)(2,1)} %all_to_all.18) | data formatting | bytes 2359296
  46.7 3.2 %copy.34 = bf16[4,64,3,768]{3,1,0,2:T(8,128)(2,1)} copy(bf16[4,64,3,768]{1,2,3,0:T(4,128)(2,1)S(1)} %bitcast.41) | data formatting | bytes 2359296 | tf_op jit(solution)/shard_map/all_to_all | solution.py:51
  49.9 0.0 copy-start
  49.9 2.2 %slice.27 = bf16[256,2,768]{2,0,1:T(8,128)(2,1)} slice(bf16[256,3,768]{2,0,1:T(8,128)(2,1)} %bitcast.43), slice={[0:256], [1:3], [0:768]} | slice | bytes 1572864 | tf_op jit(solution)/shard_map/slice | solution.py:52
  52.1 0.0 collective-permute-start
  52.1 0.0 copy-done
  52.1 0.1 fusion.13
  52.2 0.2 copy.36
  52.3 0.9 %copy.39 = bf16[256,1,768]{0,2,1:T(8,128)(2,1)} copy(bf16[256,1,768]{2,0,1:T(8,128)(2,1)S(1)} %get-tuple-element.37) | data formatting | bytes 786432 | tf_op jit(solution)/shard_map/slice | solution.py:57
  53.2 0.2 copy.35
  53.4 0.4 fusion.15
  53.8 10.9 %collective-permute-done = bf16[256,2,768]{2,0,1:T(8,128)(2,1)} collective-permute-done((bf16[256,2,768]{2,0,1:T(8,128)(2,1)}, bf16[256,2,768]{2,0,1:T(8,128)(2,1)}, u32[]{:S(2)}, u32[]{:S(2)}) %collective-permute-start) | collective-permute-done | bytes 786464 | tf_op jit(solution)/shard_map/ppermute | solution.py:13
  64.7 1.9 %fusion.14 = (bf16[256,1,768]{2,0,1:T(8,128)(2,1)}, bf16[256,1,768]{2,0,1:T(8,128)(2,1)S(1)}) fusion(bf16[256,2,768]{2,0,1:T(8,128)(2,1)} %collective-permute-done), kind=kLoop, calls=%fused_computation.21 | loop fusion | bytes 1572864 | tf_op jit(solution)/shard_map/slice | solution.py:59
  66.6 0.9 %copy.41 = bf16[256,1,768]{0,2,1:T(8,128)(2,1)} copy(bf16[256,1,768]{2,0,1:T(8,128)(2,1)S(1)} %get-tuple-element.40) | data formatting | bytes 786432 | tf_op jit(solution)/shard_map/slice | solution.py:58
  67.5 1.4 %fusion.16 = (f32[6,256]{1,0:T(8,128)S(1)}, f32[6,256,256]{1,2,0:T(8,128)S(1)}) fusion(bf16[256,6,128]{0,2,1:T(8,128)(2,1)S(1)} %bitcast.46, bf16[256,6,128]{0,2,1:T(8,128)(2,1)} %bitcast.48), kind=kOutput, calls=%fused_computation.23 | convolution fusion | flops 101448192 | bytes 2365440 | tf_op jit(solution)/shard_map/while/body/eval_jaxpr/rhd,khd->hrk/dot_general | solution.py:18
  69.0 0.0 copy-start.1
  69.0 0.4 fusion
  69.4 0.6 log_add_fusion
  70.0 0.6 bitcast_add_fusion
  70.7 0.0 copy-done.1
  70.7 0.9 %copy.44 = bf16[256,1,768]{0,2,1:T(8,128)(2,1)} copy(bf16[256,1,768]{2,0,1:T(8,128)(2,1)S(1)} %copy-done.1) | data formatting | bytes 786432 | tf_op jit(solution)/shard_map/slice | solution.py:59
  71.6 0.0 copy-start.2
  71.6 0.0 copy-start.3
  71.6 1.5 %fusion.4 = f32[256,6,128]{0,2,1:T(8,128)S(1)} fusion(bf16[256,6,128]{0,2,1:T(8,128)(2,1)} %bitcast.49, f32[6,256,256]{1,2,0:T(8,128)S(1)} %get-tuple-element.42, f32[6,256]{1,0:T(8,128)S(1)} %get-tuple-element.41, f32[256,6]{0,1:T(8,128)} %get-tuple-element.35), kind=kOutput, calls=%fused_computation.10 | convolution fusion | flops 101646336 | bytes 2764800 | tf_op jit(solution)/shard_map/while/body/eval_jaxpr/hrk,khd->hrd/dot_general | solution.py:28
  73.0 0.0 copy-done.2
  73.0 0.0 copy-done.3
  73.1 0.4 fusion.6
  73.5 1.1 %copy.46 = f32[256,768]{1,0:T(8,128)} copy(f32[256,768]{0,1:T(8,128)S(1)} %bitcast.50) | data formatting | bytes 1572864
  (1 shorter events, 0.0 us)
Async XLA Ops:
  49.9 2.2 %copy-start = (bf16[4,64,3,768]{3,1,0,2:T(8,128)(2,1)S(1)}, bf16[4,64,3,768]{3,1,0,2:T(8,128)(2,1)}, u32[]{:S(2)}) copy-start(bf16[4,64,3,768]{3,1,0,2:T(8,128)(2,1)} %copy.34) | copy-start | bytes 3538948
  52.1 12.6 %collective-permute-start = (bf16[256,2,768]{2,0,1:T(8,128)(2,1)}, bf16[256,2,768]{2,0,1:T(8,128)(2,1)}, u32[]{:S(2)}, u32[]{:S(2)}) collective-permute-start(bf16[256,2,768]{2,0,1:T(8,128)(2,1)} %slice.27), channel_id=1, source_target_pairs={{0,4},{4,8},{8,12},{12,16},{16,20},{20,24},{24,28},{28,0},{1,5},{5... | collective-permute-start | bytes 2359304 | tf_op jit(solution)/shard_map/ppermute | solution.py:13
  69.0 1.7 %copy-start.1 = (bf16[256,1,768]{2,0,1:T(8,128)(2,1)S(1)}, bf16[256,1,768]{2,0,1:T(8,128)(2,1)}, u32[]{:S(2)}) copy-start(bf16[256,1,768]{2,0,1:T(8,128)(2,1)} %get-tuple-element.39) | copy-start | bytes 1179652
  71.6 1.5 %copy-start.2 = (bf16[256,1,768]{0,2,1:T(8,128)(2,1)S(1)}, bf16[256,1,768]{0,2,1:T(8,128)(2,1)}, u32[]{:S(2)}) copy-start(bf16[256,1,768]{0,2,1:T(8,128)(2,1)} %copy.44) | copy-start | bytes 1179652
  71.6 1.5 %copy-start.3 = (f32[256,6]{0,1:T(8,128)S(1)}, f32[256,6]{0,1:T(8,128)}, u32[]{:S(2)}) copy-start(f32[256,6]{0,1:T(8,128)} %get-tuple-element.34) | copy-start | bytes 18436
where the time goes:
time: 75 us; the launch traced here: 74.6 us
  blocking collectives  35 us (47%)
  local copies, waits for them, and re-layouts  22.7 us (30%)
  waiting for transfers between devices  10.9 us (15%)
  matrix products  3.71 us (5%)
  other arithmetic  1.68 us (2%)
    all_to_all x1, blocking collectives, shards(): lax.all_to_all(qkv, 'uly', split_axis=2, concat_axis=0, tiled=True)  35 us
    unnamed x12, local copies, waits for them, and re-layouts  12.3 us
    ppermute x1, waiting for transfers between devices, from_behind(): return lax.ppermute(value, axis, pairs)  10.9 us
    all_to_all x1, local copies, waits for them, and re-layouts, shards(): lax.all_to_all(qkv, 'uly', split_axis=2, concat_axis=0, tiled=True)  3.21 us
    slice x2, local copies, waits for them, and re-layouts, shards(): prev_values = prev_pairs[:, 1].reshape(block_len, heads_local, HEAD_DIM)  2.83 us
    slice x1, local copies, waits for them, and re-layouts, shards(): prev_pairs = from_behind(grouped[:, 1:], 'blk', 1)  2.16 us
    dot_general x2, matrix products, block_scores(): jnp.einsum('rhd,khd->hrk', query_rows, key_rows, preferred_element_type=j...  1.84 us
  transfers between devices with their start and end apart: 1, of which 1 were waited for; matrix products, arithmetic and copies ran while one was open for 2% of the time, Pallas kernels for 0%

commit v1 on v0

--- a/solution.py
+++ b/solution.py
@@ -5,6 +5,13 @@
 from jax.sharding import PartitionSpec as P
 
 HEAD_DIM = 128
+
+
+def exchange_blocks(x, axis, split, join):
+    size = lax.axis_size(axis)
+    tiles = jnp.stack(jnp.split(x, size, axis=split), axis=0)
+    tiles = lax.all_to_all(tiles, axis, split_axis=0, concat_axis=0)
+    return jnp.concatenate(tiles, axis=join)
 
 
 def from_behind(value, axis, steps):
@@ -48,7 +55,7 @@
     width = qkv.shape[2] // lax.axis_size("uly")
     heads_local = width // HEAD_DIM
     temper = 1.0 / math.sqrt(HEAD_DIM)
-    grouped = lax.all_to_all(qkv, "uly", split_axis=2, concat_axis=0, tiled=True)
+    grouped = exchange_blocks(qkv, "uly", 2, 0)
     prev_pairs = from_behind(grouped[:, 1:], "blk", 1)
     block_len = grouped.shape[0]
     row_count = math.gcd(block_len, 512)

time: 75 us -> 59.4 us (0.79)
  local copies, waits for them, and re-layouts: 22.7 us -> 7.45 us
    unnamed x12 -> x7, local copies, waits for them, and re-layouts: 12.3 us -> 1.16 us
    all_to_all x1, local copies, waits for them, and re-layouts: 3.21 us -> 0.08 us  [exchange_blocks(): tiles = lax.all_to_all(tiles, axis, split_axis=0, concat_axis=0)]
    another operation x0 -> x1, local copies, waits for them, and re-layouts: none -> 1.32 us  [exchange_blocks(): tiles = jnp.stack(jnp.split(x, size, axis=split), axis=0)]
    slice x1, local copies, waits for them, and re-layouts: 2.16 us -> 0.93 us  [shards(): prev_pairs = from_behind(grouped[:, 1:], 'blk', 1)]
    slice x2, local copies, waits for them, and re-layouts: 2.83 us -> 1.71 us  [shards(): prev_values = prev_pairs[:, 1].reshape(block_len, heads_local, HEAD_DIM)]
  transfers between devices with their start and end apart: 1 -> 1, of which waited for: 1 -> 1; matrix products, arithmetic and copies ran while one was open for 2% -> 3% of each run, Pallas kernels for 0% -> 0%
where the time goes in v1:
time: 59.4 us; the launch traced here: 59.2 us
  blocking collectives  34.7 us (58%)
  waiting for transfers between devices  10.7 us (18%)
  local copies, waits for them, and re-layouts  7.45 us (13%)
  matrix products  3.72 us (6%)
  other arithmetic  1.86 us (3%)
  between operations  0.74 us (1%)
    all_to_all x1, blocking collectives, exchange_blocks(): tiles = lax.all_to_all(tiles, axis, split_axis=0, concat_axis=0)  34.7 us
    ppermute x1, waiting for transfers between devices, from_behind(): return lax.ppermute(value, axis, pairs)  10.7 us
    dot_general x2, matrix products, block_scores(): jnp.einsum('rhd,khd->hrk', query_rows, key_rows, preferred_element_type=j...  1.85 us
    slice x2, local copies, waits for them, and re-layouts, shards(): prev_values = prev_pairs[:, 1].reshape(block_len, heads_local, HEAD_DIM)  1.71 us
    dot_general x1, matrix products, attend_first(): jnp.einsum('hrk,khd->hrd', weights.astype(jnp.bfloat16), value_rows, pref...  1.45 us
    another operation x1, local copies, waits for them, and re-layouts, exchange_blocks(): tiles = jnp.stack(jnp.split(x, size, axis=split), axis=0)  1.32 us
  transfers between devices with their start and end apart: 1, of which 1 were waited for; matrix products, arithmetic and copies ran while one was open for 3% of the time, Pallas kernels for 0%

profile of v1, /device:TPU:0, one launch (start us, length us, event | category | flops | bytes accessed | tf_op | source)
XLA Modules:
  0.0 59.2 jit_solution(17559278944117453613)
XLA Ops:
  0.6 1.3 %slice_bitcast_fusion.3 = (bf16[1,64,3,768]{3,1,2,0:T(8,128)(2,1)S(1)}, bf16[1,64,3,768]{3,1,2,0:T(8,128)(2,1)S(1)}, bf16[1,64,3,768]{3,1,2,0:T(8,128)(2,1)S(1)}, bf16[1,64,3,768]{3,1,2,0:T(8,128)(2,1)S(1)}) fusion(bf16[64,3,3072]{2,0,1:T(8,128)(2,1)} %param.1), kind=kLoop, calls=%fused_computation.19 | loop fusion | bytes 2359296 | tf_op jit(solution)/shard_map/stack | solution.py:12
  2.0 0.2 pad_maximum_fusion
  2.1 34.7 %all_to_all.5 = bf16[4,64,3,768]{3,1,2,0:T(8,128)(2,1)S(1)} all-to-all(bf16[4,64,3,768]{3,1,2,0:T(8,128)(2,1)S(1)} %pad_maximum_fusion), channel_id=1, replica_groups=mesh['blk'=8,'uly'=4] {'uly'}, dimensions={0} | all-to-all | bytes 2359296 | tf_op jit(solution)/shard_map/all_to_all | solution.py:13
  36.8 0.1 copy.18
  36.9 0.9 %slice.27 = bf16[256,2,768]{2,0,1:T(8,128)(2,1)} slice(bf16[256,3,768]{2,0,1:T(8,128)(2,1)S(1)} %bitcast.43), slice={[0:256], [1:3], [0:768]} | slice | bytes 1572864 | tf_op jit(solution)/shard_map/slice | solution.py:59
  37.8 0.0 collective-permute-start
  37.8 0.1 fusion.13
  37.9 0.2 copy.20
  38.0 0.9 %copy.23 = bf16[256,1,768]{0,2,1:T(8,128)(2,1)} copy(bf16[256,1,768]{2,0,1:T(8,128)(2,1)S(1)} %get-tuple-element.35) | data formatting | bytes 786432 | tf_op jit(solution)/shard_map/slice | solution.py:64
  39.0 0.2 copy.19
  39.1 0.4 fusion.15
  39.6 10.7 %collective-permute-done = bf16[256,2,768]{2,0,1:T(8,128)(2,1)S(1)} collective-permute-done((bf16[256,2,768]{2,0,1:T(8,128)(2,1)}, bf16[256,2,768]{2,0,1:T(8,128)(2,1)S(1)}, u32[]{:S(2)}, u32[]{:S(2)}) %collective-permute-start) | collective-permute-done | bytes 786464 | tf_op jit(solution)/shard_map/ppermute | solution.py:20
  50.3 0.8 %fusion.14 = (bf16[256,1,768]{2,0,1:T(8,128)(2,1)}, bf16[256,1,768]{2,0,1:T(8,128)(2,1)S(1)}) fusion(bf16[256,2,768]{2,0,1:T(8,128)(2,1)S(1)} %collective-permute-done), kind=kLoop, calls=%fused_computation.26 | loop fusion | bytes 1572864 | tf_op jit(solution)/shard_map/slice | solution.py:66
  51.1 0.9 %copy.25 = bf16[256,1,768]{0,2,1:T(8,128)(2,1)} copy(bf16[256,1,768]{2,0,1:T(8,128)(2,1)S(1)} %get-tuple-element.42) | data formatting | bytes 786432 | tf_op jit(solution)/shard_map/slice | solution.py:65
  52.0 1.4 %fusion.16 = (f32[6,256]{1,0:T(8,128)S(1)}, f32[6,256,256]{1,2,0:T(8,128)S(1)}) fusion(bf16[256,6,128]{0,2,1:T(8,128)(2,1)S(1)} %bitcast.46, bf16[256,6,128]{0,2,1:T(8,128)(2,1)} %bitcast.48), kind=kOutput, calls=%fused_computation.28 | convolution fusion | flops 101448192 | bytes 2365440 | tf_op jit(solution)/shard_map/while/body/eval_jaxpr/rhd,khd->hrk/dot_general | solution.py:25
  53.5 0.0 copy-start
  53.5 0.5 fusion
  53.9 0.6 %log_add_fusion = f32[6,256]{1,0:T(8,128)} fusion(f32[6,256]{1,0:T(8,128)S(1)} %max.20, f32[6,256]{1,0:T(8,128)S(1)} %get-tuple-element.48, f32[6,256]{1,0:T(8,128)S(1)} %get-tuple-element.47, f32[6,256]{1,0:T(8,128)S(1)} %get-tuple-element.43), kind=kLoop, calls=%fused_computation.24 | loop fusion | flops 6144 | bytes 30720 | tf_op jit(solution)/shard_map/while/body/eval_jaxpr/add | solution.py:72
  54.6 0.6 %bitcast_add_fusion = (f32[256,6]{0,1:T(8,128)}, f32[256,6]{0,1:T(8,128)}) fusion(f32[6,256]{1,0:T(8,128)S(1)} %get-tuple-element.48, f32[6,256]{1,0:T(8,128)S(1)} %get-tuple-element.47, f32[6,256]{1,0:T(8,128)S(1)} %get-tuple-element.45, f32[6,256]{1,0:T(8,128)S(1)} %get-tuple-element.43), kind=kLoop, calls=%fused_computation.22 | loop fusion | flops 6144 | bytes 36864 | tf_op jit(solution)/shard_map/while/body/eval_jaxpr/add | solution.py:47
  55.2 0.0 copy-done
  55.2 0.9 %copy.28 = bf16[256,1,768]{0,2,1:T(8,128)(2,1)} copy(bf16[256,1,768]{2,0,1:T(8,128)(2,1)S(1)} %copy-done) | data formatting | bytes 786432 | tf_op jit(solution)/shard_map/slice | solution.py:66
  56.1 0.0 copy-start.1
  56.1 0.0 copy-start.2
  56.1 1.5 %fusion.4 = f32[256,6,128]{0,2,1:T(8,128)S(1)} fusion(bf16[256,6,128]{0,2,1:T(8,128)(2,1)} %bitcast.49, f32[6,256,256]{1,2,0:T(8,128)S(1)} %get-tuple-element.44, f32[6,256]{1,0:T(8,128)S(1)} %get-tuple-element.43, f32[256,6]{0,1:T(8,128)} %get-tuple-element.33), kind=kOutput, calls=%fused_computation.10 | convolution fusion | flops 101646336 | bytes 2764800 | tf_op jit(solution)/shard_map/while/body/eval_jaxpr/hrk,khd->hrd/dot_general | solution.py:35
  57.6 0.0 copy-done.1
  57.6 0.0 copy-done.2
  57.6 0.4 fusion.6
  58.0 1.1 %copy.30 = f32[256,768]{1,0:T(8,128)} copy(f32[256,768]{0,1:T(8,128)S(1)} %bitcast.50) | data formatting | bytes 1572864
  (1 shorter events, 0.0 us)
Async XLA Ops:
  37.8 12.5 %collective-permute-start = (bf16[256,2,768]{2,0,1:T(8,128)(2,1)}, bf16[256,2,768]{2,0,1:T(8,128)(2,1)S(1)}, u32[]{:S(2)}, u32[]{:S(2)}) collective-permute-start(bf16[256,2,768]{2,0,1:T(8,128)(2,1)} %slice.27), channel_id=1, source_target_pairs={{0,4},{4,8},{8,12},{12,16},{16,20},{20,24},{24,28},{28,0},{1,5},{5... | collective-permute-start | bytes 2359304 | tf_op jit(solution)/shard_map/ppermute | solution.py:20
  53.5 1.7 %copy-start = (bf16[256,1,768]{2,0,1:T(8,128)(2,1)S(1)}, bf16[256,1,768]{2,0,1:T(8,128)(2,1)}, u32[]{:S(2)}) copy-start(bf16[256,1,768]{2,0,1:T(8,128)(2,1)} %get-tuple-element.41) | copy-start | bytes 1179652
  56.1 1.5 %copy-start.1 = (bf16[256,1,768]{0,2,1:T(8,128)(2,1)S(1)}, bf16[256,1,768]{0,2,1:T(8,128)(2,1)}, u32[]{:S(2)}) copy-start(bf16[256,1,768]{0,2,1:T(8,128)(2,1)} %copy.28) | copy-start | bytes 1179652
  56.1 1.5 %copy-start.2 = (f32[256,6]{0,1:T(8,128)S(1)}, f32[256,6]{0,1:T(8,128)}, u32[]{:S(2)}) copy-start(f32[256,6]{0,1:T(8,128)} %get-tuple-element.32) | copy-start | bytes 18436
